TPU v7x, 32 devices: a whole 2x2x4 slice. The times are simulated.
32 devices in a mesh: groups: 2 (over x), dev: 8 (over z, y), sub: 2 (over core).
Axes of the slice: x: 2, y: 2, z: 4, core: 2. Of those that a mesh axis runs over, the one named last changes fastest.
Arguments:
- hidden: bfloat16 [128, 6144], P(('groups', 'dev')), parts along dimension 0, may hold values from -6 to 6
- query: bfloat16 [128, 48, 128], P(('groups', 'dev'), 'sub'), parts along dimension 0, may hold values from -180 to 180
- cache_keys: bfloat16 [128, 8, 64, 128], P(('groups', 'dev'), 'sub'), parts along dimension 0, may hold values from -6 to 6
- cache_values: bfloat16 [128, 8, 64, 128], P(('groups', 'dev'), 'sub'), parts along dimension 0, may hold values from -6 to 6
- lengths: int32 [128], P(('groups', 'dev')), parts along dimension 0, may hold values from 16 to 64
- out_proj: bfloat16 [6144, 6144], P('sub', 'dev'), may hold values from -0.078125 to 0.078125
- norm_gain: float32 [6144], replicated, may hold values from 0.1 to 1.9
- router: bfloat16 [6144, 4], replicated, may hold values from -0.078125 to 0.078125
- low_factor: bfloat16 [6144, 256], P('sub'), may hold values from -0.078125 to 0.078125
- gate_weight: bfloat16 [6144, 32768], P(None, ('dev', 'sub')), may hold values from -0.078125 to 0.078125
- up_weight: bfloat16 [6144, 32768], P(None, ('dev', 'sub')), may hold values from -0.078125 to 0.078125
- down_weight: bfloat16 [32768, 6144], P(('dev', 'sub')), may hold values from -0.0625 to 0.0625
- gate_low: bfloat16 [256, 32768], P(None, ('dev', 'sub')), may hold values from -0.375 to 0.375
- up_low: bfloat16 [256, 32768], P(None, ('dev', 'sub')), may hold values from -0.375 to 0.375
- experts: int32 [128, 2], P(('groups', 'dev')), parts along dimension 0, may hold values from 0 to 3, all different within a row; in each aligned block of 8 rows (0 to 7, 8 to 15, ...) at most 6 rows name the same one
Outputs:
- layer_out: bfloat16 [128, 6144], P(('groups', 'dev')), parts along dimension 0
- mixture: float32 [128, 6144], P(('groups', 'dev')), parts along dimension 0
There are 2 independent parts, one for each index of `groups`. A program takes and returns all parts, laid end to end along the dimension named above; an argument that names none is the same for every part. Nothing has to cross between parts.
Inputs may be any that keep to these rules, and one draw needn't show every extreme that they name: Each row names two different experts. Among the 8 requests of one device no expert is named more than 6 times, and that bound is reached on some device.
All inputs are finite; a program needn't handle non-finite values.
Results may differ from a plain program's by a relative error of at most 0.015.
Values may be sent and summed in bfloat16 or wider, within the bound.
A program may use at most 128 MiB of HBM per device.

v0:
```python
import jax
import jax.numpy as jnp
from jax import lax
from jax.sharding import PartitionSpec as P

CAP = 6
EPSILON = 1e-05


def expert_shard(row_block, low_rank, gate_weight, up_weight, down_weight, gate_low, up_low):
    gate_sum = jnp.dot(row_block, gate_weight, preferred_element_type=jnp.float32) + jnp.dot(
        low_rank, gate_low, preferred_element_type=jnp.float32
    )
    up_sum = jnp.dot(row_block, up_weight, preferred_element_type=jnp.float32) + jnp.dot(
        low_rank, up_low, preferred_element_type=jnp.float32
    )
    inner_act = (jax.nn.silu(gate_sum) * up_sum).astype(jnp.bfloat16)
    return jnp.dot(inner_act, down_weight, preferred_element_type=jnp.float32)


def route_gates(normed, router, experts):
    logits = jnp.dot(normed, router, preferred_element_type=jnp.float32)
    labels = lax.broadcasted_iota(jnp.int32, (1, 1, router.shape[1]), 2)
    picked = (experts[:, :, None] == labels).astype(jnp.float32)
    chosen = jnp.sum(logits[:, None, :] * picked, axis=-1)
    leading = jax.nn.sigmoid(chosen[:, 0] - chosen[:, 1])
    return jnp.stack([leading, 1.0 - leading], axis=-1)


def body(
    hidden,
    query,
    cache_keys,
    cache_values,
    lengths,
    out_proj,
    norm_gain,
    router,
    low_factor,
    gate_weight,
    up_weight,
    down_weight,
    gate_low,
    up_low,
    experts,
):
    requests = hidden.shape[0]
    model_width = hidden.shape[1]
    heads_here = query.shape[1]
    kv_here = cache_keys.shape[1]
    span_len = cache_keys.shape[2]
    head_size = query.shape[2]
    grouped = query.reshape(requests, kv_here, heads_here // kv_here, head_size)
    scores = jnp.einsum(
        "rkgd,rkld->rkgl", grouped, cache_keys, preferred_element_type=jnp.float32
    ) * head_size ** (-0.5)
    visible = lax.broadcasted_iota(jnp.int32, (requests, span_len), 1) < lengths[:, None]
    scores = jnp.where(visible[:, None, None, :], scores, -1e30)
    attn_probs = jax.nn.softmax(scores, axis=-1).astype(jnp.bfloat16)
    attended = jnp.einsum(
        "rkgl,rkld->rkgd", attn_probs, cache_values, preferred_element_type=jnp.float32
    )
    attended = attended.astype(jnp.bfloat16).reshape(requests, heads_here * head_size)
    columns = jnp.dot(
        lax.all_gather(attended, "dev", axis=0, tiled=True),
        out_proj,
        preferred_element_type=jnp.float32,
    )
    partial_proj = lax.all_to_all(columns, "dev", split_axis=0, concat_axis=1, tiled=True)
    residual = hidden.astype(jnp.float32) + lax.psum(partial_proj, "sub")
    inverse = lax.rsqrt(jnp.mean(residual * residual, axis=-1, keepdims=True) + EPSILON)
    normed = (residual * inverse * norm_gain).astype(jnp.bfloat16)
    half_width = low_factor.shape[0]
    normed_half = lax.dynamic_slice_in_dim(
        normed, lax.axis_index("sub") * half_width, half_width, 1
    )
    low_partial = jnp.dot(normed_half, low_factor, preferred_element_type=jnp.float32)
    low_rank = lax.psum(low_partial, "sub").astype(jnp.bfloat16)
    rank_width = low_rank.shape[1]
    expert_count = router.shape[1]
    holders = lax.axis_size("dev") // expert_count
    gate_pair = route_gates(normed, router, experts)
    flat_ids = experts.reshape(-1)
    entries = flat_ids.shape[0]
    same_expert = flat_ids[:, None] == flat_ids[None, :]
    earlier = lax.broadcasted_iota(jnp.int32, (entries, entries), 0) > lax.broadcasted_iota(
        jnp.int32, (entries, entries), 1
    )
    slot_index = jnp.sum((same_expert & earlier).astype(jnp.int32), axis=1).reshape(requests, 2)
    target = experts * CAP + slot_index
    placement = (
        target[:, :, None] == lax.broadcasted_iota(jnp.int32, (1, 1, expert_count * CAP), 2)
    ).astype(jnp.float32)
    chosen = jnp.sum(placement, axis=1).astype(jnp.bfloat16)
    packed_rows = jnp.einsum(
        "rs,rd->sd", chosen, normed, preferred_element_type=jnp.float32
    ).astype(jnp.bfloat16)
    packed_low = jnp.einsum(
        "rs,rd->sd", chosen, low_rank, preferred_element_type=jnp.float32
    ).astype(jnp.bfloat16)
    send_rows = jnp.repeat(packed_rows.reshape(expert_count, CAP, model_width), holders, axis=0)
    send_low = jnp.repeat(packed_low.reshape(expert_count, CAP, rank_width), holders, axis=0)
    got_rows = lax.all_to_all(send_rows, "dev", split_axis=0, concat_axis=0, tiled=True)
    got_low = lax.all_to_all(send_low, "dev", split_axis=0, concat_axis=0, tiled=True)
    sources = got_rows.shape[0]
    slot_count = got_rows.shape[1]
    result = expert_shard(
        got_rows.reshape(sources * slot_count, model_width),
        got_low.reshape(sources * slot_count, rank_width),
        gate_weight,
        up_weight,
        down_weight,
        gate_low,
        up_low,
    )
    partials = result.reshape(sources, slot_count, model_width)
    returned = lax.all_to_all(
        partials.astype(jnp.bfloat16), "dev", split_axis=0, concat_axis=0, tiled=True
    ).astype(partials.dtype)
    per_slot = jnp.sum(returned.reshape(expert_count, holders, CAP, model_width), axis=1).reshape(
        expert_count * CAP, model_width
    )
    weighted = jnp.sum(placement * gate_pair[:, :, None], axis=1)
    mixture_part = jnp.dot(weighted, per_slot, precision=lax.Precision.HIGHEST)
    mixture = lax.psum(mixture_part.astype(jnp.bfloat16), "sub").astype(jnp.float32)
    return ((residual + mixture).astype(jnp.bfloat16), mixture)


def solution(mesh):
    placed = (
        P(("groups", "dev"), None),
        P(("groups", "dev"), "sub", None),
        P(("groups", "dev"), "sub", None, None),
        P(("groups", "dev"), "sub", None, None),
        P(("groups", "dev")),
        P("sub", "dev"),
        P(),
        P(),
        P("sub", None),
        P(None, ("dev", "sub")),
        P(None, ("dev", "sub")),
        P(("dev", "sub"), None),
        P(None, ("dev", "sub")),
        P(None, ("dev", "sub")),
        P(("groups", "dev"), None),
    )
    return jax.shard_map(
        body,
        mesh=mesh,
        in_specs=placed,
        out_specs=(P(("groups", "dev"), None), P(("groups", "dev"), None)),
        check_vma=False,
    )
```

profile of v0, /device:TPU:0, one launch (start us, length us, event | category | flops | bytes accessed | tf_op | source)
XLA Modules:
  0.0 208.5 jit_solution(1701919824446412445)
XLA Ops:
  8.8 1.4 fusion.4
  10.5 1.6 convolution_convert_fusion.3
  12.1 32.8 %all_gather.3 = bf16[64,3072]{1,0:T(8,128)(2,1)S(1)} all-gather(bf16[8,3072]{1,0:T(8,128)(2,1)S(1)} %reshape.78), channel_id=1, replica_groups=mesh['groups'=2,'dev'=8,'sub'=2] {'dev'}, dimensions={0}, use_global_device_ids=true | all-gather | bytes 442368 | tf_op jit(solution)/shard_map/all_gather | solution.py:65
  44.9 3.9 %convolution_bitcast_fusion = f32[8,8,768]{2,1,0:T(8,128)} fusion(bf16[64,3072]{1,0:T(8,128)(2,1)S(1)} %all_gather.3, bf16[3072,768]{1,0:T(8,128)(2,1)} %param.20), kind=kOutput, calls=%fused_computation.9 | convolution fusion | flops 301989888 | bytes 5308416 | tf_op jit(solution)/shard_map/dot_general | solution.py:64
  48.8 5.7 %all-to-all-start = ((f32[8,8,768]{2,1,0:T(8,128)}), f32[8,8,768]{2,1,0:T(8,128)S(1)}, u32[]{:S(2)}, u32[]{:S(2)}) async-start(f32[8,8,768]{2,1,0:T(8,128)} %convolution_bitcast_fusion), calls=%async_computation | async-start | bytes 393216 | tf_op jit(solution)/shard_map/all_to_all | solution.py:69
  55.6 6.6 %all-to-all-done = f32[8,8,768]{2,1,0:T(8,128)S(1)} async-done(((f32[8,8,768]{2,1,0:T(8,128)}), f32[8,8,768]{2,1,0:T(8,128)S(1)}, u32[]{:S(2)}, u32[]{:S(2)}) %all-to-all-start) | async-done | bytes 196640 | tf_op jit(solution)/shard_map/all_to_all | solution.py:69
  63.1 16.1 %all-reduce.3.cloned.1.call-done = f32[8,6144]{1,0:T(8,128)} async-done(((f32[8,6144]{1,0:T(8,128)}), f32[8,6144]{1,0:T(8,128)}) %all-reduce.3.cloned.1.call-update) | async-done | bytes 196624 | tf_op jit(solution)/shard_map/psum | solution.py:70
  79.2 1.2 multiply_reduce_fusion
  80.4 1.1 multiply_convert_fusion
  81.5 1.0 fusion.23
  83.5 2.5 %psum.22 = bf16[8,256]{1,0:T(8,128)(2,1)S(1)} all-reduce(f32[8,256]{1,0:T(8,128)S(1)} %fusion.14), channel_id=1, replica_groups=mesh['groups'=2,'dev'=8,'sub'=2] {'sub'}, use_global_device_ids=true, to_apply=%region_8.9 | all-reduce | flops 2048 | bytes 12288 | tf_op jit(solution)/shard_map/psum | solution.py:78
  86.9 5.8 %all-to-all-start.2 = ((bf16[8,6,256]{2,1,0:T(8,128)(2,1)}), bf16[8,6,256]{2,1,0:T(8,128)(2,1)S(1)}, u32[]{:S(2)}, u32[]{:S(2)}) async-start(bf16[8,6,256]{2,1,0:T(8,128)(2,1)} %bitcast.5), calls=%async_computation.2 | async-start | bytes 65536 | tf_op jit(solution)/shard_map/all_to_all | solution.py:104
  93.1 6.3 %all-to-all-done.2 = bf16[8,6,256]{2,1,0:T(8,128)(2,1)S(1)} async-done(((bf16[8,6,256]{2,1,0:T(8,128)(2,1)}), bf16[8,6,256]{2,1,0:T(8,128)(2,1)S(1)}, u32[]{:S(2)}, u32[]{:S(2)}) %all-to-all-start.2) | async-done | bytes 24608 | tf_op jit(solution)/shard_map/all_to_all | solution.py:104
  99.4 0.9 broadcast_in_dim.18
  100.3 3.5 %all-to-all-start.1 = ((bf16[8,6,6144]{2,1,0:T(8,128)(2,1)}), bf16[8,6,6144]{2,1,0:T(8,128)(2,1)S(1)}, u32[]{:S(2)}, u32[]{:S(2)}) async-start(bf16[8,6,6144]{2,1,0:T(8,128)(2,1)} %bitcast.4), calls=%async_computation.1 | async-start | bytes 1572864 | tf_op jit(solution)/shard_map/all_to_all | solution.py:103
  103.9 19.4 %all-to-all-done.1 = bf16[8,6,6144]{2,1,0:T(8,128)(2,1)S(1)} async-done(((bf16[8,6,6144]{2,1,0:T(8,128)(2,1)}), bf16[8,6,6144]{2,1,0:T(8,128)(2,1)S(1)}, u32[]{:S(2)}, u32[]{:S(2)}) %all-to-all-start.1) | async-done | bytes 589856 | tf_op jit(solution)/shard_map/all_to_all | solution.py:103
  123.6 10.5 %fusion.25 = f32[48,2048]{1,0:T(8,128)S(1)} fusion(bf16[48,6144]{1,0:T(8,128)(2,1)S(1)} %reshape.82, bf16[6144,2048]{1,0:T(8,128)(2,1)} %param.25), kind=kOutput, calls=%fused_computation.53 | convolution fusion | flops 1207959552 | bytes 26148864 | tf_op jit(solution)/shard_map/dot_general | solution.py:14
  134.2 10.5 %fusion.24 = f32[48,2048]{1,0:T(8,128)S(1)} fusion(bf16[48,6144]{1,0:T(8,128)(2,1)S(1)} %reshape.82, bf16[6144,2048]{1,0:T(8,128)(2,1)} %param.24), kind=kOutput, calls=%fused_computation.52 | convolution fusion | flops 1207959552 | bytes 26148864 | tf_op jit(solution)/shard_map/dot_general | solution.py:11
  145.1 11.6 %convolution_convert_fusion = bf16[48,6144]{1,0:T(8,128)(2,1)} fusion(bf16[2048,6144]{1,0:T(8,128)(2,1)} %param.26, f32[48,2048]{1,0:T(8,128)S(1)} %fusion.25, bf16[48,256]{1,0:T(8,128)(2,1)S(1)} %reshape.85, bf16[256,2048]{1,0:T(8,128)(2,1)S(1)} %copy-done.2, f32[48,2048]{1,0:T(8,128)S(1)} %convolution_add_fusion.1), kind=kOutput, calls=%fused_computation.1 | convolution fusion | flops 1259274240 | bytes 27615232 | tf_op jit(solution)/shard_map/dot_general | solution.py:18
  156.7 1.3 convert_element_type.62
  158.0 23.6 %all_to_all.34 = bf16[8,6,6144]{2,1,0:T(8,128)(2,1)S(1)} all-to-all(bf16[8,6,6144]{2,1,0:T(8,128)(2,1)S(1)} %convert_element_type.62), channel_id=1, replica_groups=mesh['groups'=2,'dev'=8,'sub'=2] {'dev'}, dimensions={0} | all-to-all | bytes 1179648 | tf_op jit(solution)/shard_map/all_to_all | solution.py:117
  181.8 1.1 convolution_convert_fusion.2
  182.9 17.0 %all-reduce.5.cloned.1.call-done = bf16[8,6144]{1,0:T(8,128)(2,1)} async-done(((bf16[8,6144]{1,0:T(8,128)(2,1)}), bf16[8,6144]{1,0:T(8,128)(2,1)}) %all-reduce.5.cloned.1.call-update) | async-done | bytes 98320 | tf_op jit(solution)/shard_map/psum | solution.py:125
  199.9 1.7 add_convert_fusion
  (42 shorter events, 7.1 us)
Async XLA Ops:
  7.2 76.0 %copy-start = (bf16[3072,256]{1,0:T(8,128)(2,1)S(1)}, bf16[3072,256]{1,0:T(8,128)(2,1)}, u32[]{:S(2)}) copy-start(bf16[3072,256]{1,0:T(8,128)(2,1)} %param.23) | copy-start | bytes 4718596
  48.8 13.4 %all-to-all-start = ((f32[8,8,768]{2,1,0:T(8,128)}), f32[8,8,768]{2,1,0:T(8,128)S(1)}, u32[]{:S(2)}, u32[]{:S(2)}) async-start(f32[8,8,768]{2,1,0:T(8,128)} %convolution_bitcast_fusion), calls=%async_computation | async-start | bytes 393216 | tf_op jit(solution)/shard_map/all_to_all | solution.py:69
  54.5 24.7 %all-reduce.3.cloned.1.call-start = ((), (), s32[]{:S(2)}) async-start(), calls=%async_computation.4 | async-start | bytes 393216 | tf_op jit(solution)/shard_map/psum | solution.py:70
  62.3 0.7 copy-start.5
  86.9 12.5 %all-to-all-start.2 = ((bf16[8,6,256]{2,1,0:T(8,128)(2,1)}), bf16[8,6,256]{2,1,0:T(8,128)(2,1)S(1)}, u32[]{:S(2)}, u32[]{:S(2)}) async-start(bf16[8,6,256]{2,1,0:T(8,128)(2,1)} %bitcast.5), calls=%async_computation.2 | async-start | bytes 65536 | tf_op jit(solution)/shard_map/all_to_all | solution.py:104
  100.3 23.1 %all-to-all-start.1 = ((bf16[8,6,6144]{2,1,0:T(8,128)(2,1)}), bf16[8,6,6144]{2,1,0:T(8,128)(2,1)S(1)}, u32[]{:S(2)}, u32[]{:S(2)}) async-start(bf16[8,6,6144]{2,1,0:T(8,128)(2,1)} %bitcast.4), calls=%async_computation.1 | async-start | bytes 1572864 | tf_op jit(solution)/shard_map/all_to_all | solution.py:103
  103.9 96.1 %all-reduce.5.cloned.1.call-start = ((), (), s32[]{:S(2)}) async-start(), calls=%async_computation.5 | async-start | bytes 196608 | tf_op jit(solution)/shard_map/psum | solution.py:125
  123.6 21.1 %copy-start.3 = (bf16[256,2048]{1,0:T(8,128)(2,1)S(1)}, bf16[256,2048]{1,0:T(8,128)(2,1)}, u32[]{:S(2)}) copy-start(bf16[256,2048]{1,0:T(8,128)(2,1)} %param.27) | copy-start | bytes 3145732
  134.2 10.9 %copy-start.2 = (bf16[256,2048]{1,0:T(8,128)(2,1)S(1)}, bf16[256,2048]{1,0:T(8,128)(2,1)}, u32[]{:S(2)}) copy-start(bf16[256,2048]{1,0:T(8,128)(2,1)} %param.28) | copy-start | bytes 3145732
  144.7 56.9 %copy-start.1 = (bf16[3072,256]{1,0:T(8,128)(2,1)S(1)}, bf16[3072,256]{1,0:T(8,128)(2,1)}, u32[]{:S(2)}) copy-start(bf16[3072,256]{1,0:T(8,128)(2,1)} %param.23) | copy-start | bytes 4718596
  145.1 54.9 %copy-start.4 = (bf16[8,6144]{1,0:T(8,128)(2,1)S(1)}, bf16[8,6144]{1,0:T(8,128)(2,1)}, u32[]{:S(2)}) copy-start(bf16[8,6144]{1,0:T(8,128)(2,1)} %param.15) | copy-start | bytes 294916
Sparse Core Ops, SparseCore 0:
  63.1 16.0 all-reduce.2
  183.0 16.8 all-reduce.4
where the time goes:
time: 209 us; the launch traced here: 208 us
  waiting for transfers between devices  65.5 us (31%)
  blocking collectives  58.9 us (28%)
  matrix products  42.7 us (20%)
  starting transfers between devices  15.1 us (7%)
  between operations  14.2 us (7%)
  other arithmetic  6.22 us (3%)
  local copies, waits for them, and re-layouts  5.86 us (3%)
    all_gather x1, blocking collectives, body(): lax.all_gather(attended, 'dev', axis=0, tiled=True)  32.8 us
    all_to_all x1, blocking collectives, body(): lax.all_to_all(partials.astype(jnp.bfloat16), 'dev', split_axis=0, concat...  23.6 us
    all_to_all x1, waiting for transfers between devices, body(): lax.all_to_all(send_rows, 'dev', split_axis=0, concat_axis=0, tiled=True)  19.4 us
    psum x1, waiting for transfers between devices, body(): lax.psum(mixture_part.astype(jnp.bfloat16), 'sub').astype(jnp.float32)  17 us
    psum x1, waiting for transfers between devices, body(): residual = hidden.astype(jnp.float32) + lax.psum(partial_proj, 'sub')  16.1 us
    dot_general x1, matrix products, expert_shard(): return jnp.dot(inner_act, down_weight, preferred_element_type=jnp.float32)  11.6 us
    dot_general x1, matrix products, expert_shard(): jnp.dot(row_block, up_weight, preferred_element_type=jnp.float32)  10.5 us
    dot_general x1, matrix products, expert_shard(): jnp.dot(row_block, gate_weight, preferred_element_type=jnp.float32)  10.5 us
  transfers between devices with their start and end apart: 5, of which 5 were waited for; matrix products, arithmetic and copies ran while one was open for 1% of the time, Pallas kernels for 0%

commit v1 on v0

--- a/solution.py
+++ b/solution.py
@@ -122,7 +122,9 @@
     )
     weighted = jnp.sum(placement * gate_pair[:, :, None], axis=1)
     mixture_part = jnp.dot(weighted, per_slot, precision=lax.Precision.HIGHEST)
-    mixture = lax.psum(mixture_part.astype(jnp.bfloat16), "sub").astype(jnp.float32)
+    mixture = jnp.sum(lax.all_gather(mixture_part.astype(jnp.bfloat16), "sub"), axis=0).astype(
+        jnp.float32
+    )
     return ((residual + mixture).astype(jnp.bfloat16), mixture)
 
 

time: 209 us -> 194 us (0.928)
  waiting for transfers between devices: 65.5 us -> 48.6 us
    psum x1 -> x0, waiting for transfers between devices: 17 us -> none  [body(): lax.psum(mixture_part.astype(jnp.bfloat16), 'sub').astype(jnp.float32)]
  transfers between devices with their start and end apart: 5 -> 4, of which waited for: 5 -> 4; matrix products, arithmetic and copies ran while one was open for 1% -> 1% of each run, Pallas kernels for 0% -> 0%
where the time goes in v1:
time: 194 us; the launch traced here: 193 us
  blocking collectives  60.8 us (31%)
  waiting for transfers between devices  48.6 us (25%)
  matrix products  42.1 us (22%)
  starting transfers between devices  15.1 us (8%)
  between operations  14.2 us (7%)
  other arithmetic  6.19 us (3%)
  local copies, waits for them, and re-layouts  5.86 us (3%)
    all_gather x1, blocking collectives, body(): lax.all_gather(attended, 'dev', axis=0, tiled=True)  32.8 us
    all_to_all x1, blocking collectives, body(): lax.all_to_all(partials.astype(jnp.bfloat16), 'dev', split_axis=0, concat...  23.6 us
    all_to_all x1, waiting for transfers between devices, body(): lax.all_to_all(send_rows, 'dev', split_axis=0, concat_axis=0, tiled=True)  19.5 us
    psum x1, waiting for transfers between devices, body(): residual = hidden.astype(jnp.float32) + lax.psum(partial_proj, 'sub')  16.1 us
    dot_general x1, matrix products, expert_shard(): return jnp.dot(inner_act, down_weight, preferred_element_type=jnp.float32)  11.6 us
    dot_general x1, matrix products, expert_shard(): jnp.dot(row_block, up_weight, preferred_element_type=jnp.float32)  10.5 us
    dot_general x1, matrix products, expert_shard(): jnp.dot(row_block, gate_weight, preferred_element_type=jnp.float32)  10.5 us
    all_to_all x1, waiting for transfers between devices, body(): lax.all_to_all(columns, 'dev', split_axis=0, concat_axis=1, tiled=True)  6.63 us
  transfers between devices with their start and end apart: 4, of which 4 were waited for; matrix products, arithmetic and copies ran while one was open for 1% of the time, Pallas kernels for 0%

profile of v1, /device:TPU:0, one launch (start us, length us, event | category | flops | bytes accessed | tf_op | source)
XLA Modules:
  0.0 192.8 jit_solution(79586320034067857)
XLA Ops:
  7.2 0.8 iota_compare_fusion.3
  8.8 1.4 fusion.4
  10.5 1.6 convolution_convert_fusion.3
  12.1 32.8 %all_gather.9 = bf16[64,3072]{1,0:T(8,128)(2,1)S(1)} all-gather(bf16[8,3072]{1,0:T(8,128)(2,1)S(1)} %reshape.78), channel_id=1, replica_groups=mesh['groups'=2,'dev'=8,'sub'=2] {'dev'}, dimensions={0}, use_global_device_ids=true | all-gather | bytes 442368 | tf_op jit(solution)/shard_map/all_gather | solution.py:65
  44.9 3.9 %convolution_bitcast_fusion = f32[8,8,768]{2,1,0:T(8,128)} fusion(bf16[64,3072]{1,0:T(8,128)(2,1)S(1)} %all_gather.9, bf16[3072,768]{1,0:T(8,128)(2,1)} %param.20), kind=kOutput, calls=%fused_computation.9 | convolution fusion | flops 301989888 | bytes 5308416 | tf_op jit(solution)/shard_map/dot_general | solution.py:64
  48.8 5.7 %all-to-all-start = ((f32[8,8,768]{2,1,0:T(8,128)}), f32[8,8,768]{2,1,0:T(8,128)S(1)}, u32[]{:S(2)}, u32[]{:S(2)}) async-start(f32[8,8,768]{2,1,0:T(8,128)} %convolution_bitcast_fusion), calls=%async_computation | async-start | bytes 393216 | tf_op jit(solution)/shard_map/all_to_all | solution.py:69
  55.6 6.6 %all-to-all-done = f32[8,8,768]{2,1,0:T(8,128)S(1)} async-done(((f32[8,8,768]{2,1,0:T(8,128)}), f32[8,8,768]{2,1,0:T(8,128)S(1)}, u32[]{:S(2)}, u32[]{:S(2)}) %all-to-all-start) | async-done | bytes 196640 | tf_op jit(solution)/shard_map/all_to_all | solution.py:69
  63.1 16.1 %all-reduce.2.cloned.1.call-done = f32[8,6144]{1,0:T(8,128)} async-done(((f32[8,6144]{1,0:T(8,128)}), f32[8,6144]{1,0:T(8,128)}) %all-reduce.2.cloned.1.call-update) | async-done | bytes 196624 | tf_op jit(solution)/shard_map/psum | solution.py:70
  79.2 1.2 multiply_reduce_fusion
  80.4 1.1 multiply_convert_fusion
  81.5 1.0 fusion.23
  83.5 2.5 %psum.15 = bf16[8,256]{1,0:T(8,128)(2,1)S(1)} all-reduce(f32[8,256]{1,0:T(8,128)S(1)} %fusion.14), channel_id=1, replica_groups=mesh['groups'=2,'dev'=8,'sub'=2] {'sub'}, use_global_device_ids=true, to_apply=%region_8.9 | all-reduce | flops 2048 | bytes 12288 | tf_op jit(solution)/shard_map/psum | solution.py:78
  86.9 5.8 %all-to-all-start.2 = ((bf16[8,6,256]{2,1,0:T(8,128)(2,1)}), bf16[8,6,256]{2,1,0:T(8,128)(2,1)S(1)}, u32[]{:S(2)}, u32[]{:S(2)}) async-start(bf16[8,6,256]{2,1,0:T(8,128)(2,1)} %bitcast.5), calls=%async_computation.2 | async-start | bytes 65536 | tf_op jit(solution)/shard_map/all_to_all | solution.py:104
  93.1 6.3 %all-to-all-done.2 = bf16[8,6,256]{2,1,0:T(8,128)(2,1)S(1)} async-done(((bf16[8,6,256]{2,1,0:T(8,128)(2,1)}), bf16[8,6,256]{2,1,0:T(8,128)(2,1)S(1)}, u32[]{:S(2)}, u32[]{:S(2)}) %all-to-all-start.2) | async-done | bytes 24608 | tf_op jit(solution)/shard_map/all_to_all | solution.py:104
  99.4 0.9 broadcast_in_dim.18
  100.3 3.5 %all-to-all-start.1 = ((bf16[8,6,6144]{2,1,0:T(8,128)(2,1)}), bf16[8,6,6144]{2,1,0:T(8,128)(2,1)S(1)}, u32[]{:S(2)}, u32[]{:S(2)}) async-start(bf16[8,6,6144]{2,1,0:T(8,128)(2,1)} %bitcast.4), calls=%async_computation.1 | async-start | bytes 1572864 | tf_op jit(solution)/shard_map/all_to_all | solution.py:103
  103.9 19.5 %all-to-all-done.1 = bf16[8,6,6144]{2,1,0:T(8,128)(2,1)S(1)} async-done(((bf16[8,6,6144]{2,1,0:T(8,128)(2,1)}), bf16[8,6,6144]{2,1,0:T(8,128)(2,1)S(1)}, u32[]{:S(2)}, u32[]{:S(2)}) %all-to-all-start.1) | async-done | bytes 589856 | tf_op jit(solution)/shard_map/all_to_all | solution.py:103
  123.6 10.5 %fusion.25 = f32[48,2048]{1,0:T(8,128)S(1)} fusion(bf16[48,6144]{1,0:T(8,128)(2,1)S(1)} %reshape.82, bf16[6144,2048]{1,0:T(8,128)(2,1)} %param.25), kind=kOutput, calls=%fused_computation.54 | convolution fusion | flops 1207959552 | bytes 26148864 | tf_op jit(solution)/shard_map/dot_general | solution.py:14
  134.2 10.5 %fusion.24 = f32[48,2048]{1,0:T(8,128)S(1)} fusion(bf16[48,6144]{1,0:T(8,128)(2,1)S(1)} %reshape.82, bf16[6144,2048]{1,0:T(8,128)(2,1)} %param.24), kind=kOutput, calls=%fused_computation.53 | convolution fusion | flops 1207959552 | bytes 26148864 | tf_op jit(solution)/shard_map/dot_general | solution.py:11
  145.1 11.6 %convolution_convert_fusion = bf16[48,6144]{1,0:T(8,128)(2,1)} fusion(bf16[2048,6144]{1,0:T(8,128)(2,1)} %param.26, f32[48,2048]{1,0:T(8,128)S(1)} %fusion.25, bf16[48,256]{1,0:T(8,128)(2,1)S(1)} %reshape.85, bf16[256,2048]{1,0:T(8,128)(2,1)S(1)} %copy-done.2, f32[48,2048]{1,0:T(8,128)S(1)} %convolution_add_fusion.1), kind=kOutput, calls=%fused_computation.1 | convolution fusion | flops 1259274240 | bytes 27615232 | tf_op jit(solution)/shard_map/dot_general | solution.py:18
  156.7 1.3 convert_element_type.64
  158.0 23.6 %all_to_all.34 = bf16[8,6,6144]{2,1,0:T(8,128)(2,1)S(1)} all-to-all(bf16[8,6,6144]{2,1,0:T(8,128)(2,1)S(1)} %convert_element_type.64), channel_id=1, replica_groups=mesh['groups'=2,'dev'=8,'sub'=2] {'dev'}, dimensions={0} | all-to-all | bytes 1179648 | tf_op jit(solution)/shard_map/all_to_all | solution.py:117
  182.3 1.9 %all-gather = bf16[16,6144]{1,0:T(8,128)(2,1)S(1)} all-gather(bf16[8,6144]{1,0:T(8,128)(2,1)S(1)} %convolution_convert_fusion.2), channel_id=2, replica_groups=mesh['groups'=2,'dev'=8,'sub'=2] {'sub'}, dimensions={0}, use_global_device_ids=true | all-gather | bytes 294912 | tf_op jit(solution)/shard_map/all_gather | solution.py:125
  184.2 1.7 add_convert_fusion
  (41 shorter events, 6.6 us)
Async XLA Ops:
  7.2 76.0 %copy-start = (bf16[3072,256]{1,0:T(8,128)(2,1)S(1)}, bf16[3072,256]{1,0:T(8,128)(2,1)}, u32[]{:S(2)}) copy-start(bf16[3072,256]{1,0:T(8,128)(2,1)} %param.23) | copy-start | bytes 4718596
  48.8 13.4 %all-to-all-start = ((f32[8,8,768]{2,1,0:T(8,128)}), f32[8,8,768]{2,1,0:T(8,128)S(1)}, u32[]{:S(2)}, u32[]{:S(2)}) async-start(f32[8,8,768]{2,1,0:T(8,128)} %convolution_bitcast_fusion), calls=%async_computation | async-start | bytes 393216 | tf_op jit(solution)/shard_map/all_to_all | solution.py:69
  54.5 24.7 %all-reduce.2.cloned.1.call-start = ((), (), s32[]{:S(2)}) async-start(), calls=%async_computation.4 | async-start | bytes 393216 | tf_op jit(solution)/shard_map/psum | solution.py:70
  62.3 0.7 copy-start.5
  86.9 12.5 %all-to-all-start.2 = ((bf16[8,6,256]{2,1,0:T(8,128)(2,1)}), bf16[8,6,256]{2,1,0:T(8,128)(2,1)S(1)}, u32[]{:S(2)}, u32[]{:S(2)}) async-start(bf16[8,6,256]{2,1,0:T(8,128)(2,1)} %bitcast.5), calls=%async_computation.2 | async-start | bytes 65536 | tf_op jit(solution)/shard_map/all_to_all | solution.py:104
  100.3 23.1 %all-to-all-start.1 = ((bf16[8,6,6144]{2,1,0:T(8,128)(2,1)}), bf16[8,6,6144]{2,1,0:T(8,128)(2,1)S(1)}, u32[]{:S(2)}, u32[]{:S(2)}) async-start(bf16[8,6,6144]{2,1,0:T(8,128)(2,1)} %bitcast.4), calls=%async_computation.1 | async-start | bytes 1572864 | tf_op jit(solution)/shard_map/all_to_all | solution.py:103
  123.6 21.1 %copy-start.3 = (bf16[256,2048]{1,0:T(8,128)(2,1)S(1)}, bf16[256,2048]{1,0:T(8,128)(2,1)}, u32[]{:S(2)}) copy-start(bf16[256,2048]{1,0:T(8,128)(2,1)} %param.27) | copy-start | bytes 3145732
  134.2 10.9 %copy-start.2 = (bf16[256,2048]{1,0:T(8,128)(2,1)S(1)}, bf16[256,2048]{1,0:T(8,128)(2,1)}, u32[]{:S(2)}) copy-start(bf16[256,2048]{1,0:T(8,128)(2,1)} %param.28) | copy-start | bytes 3145732
  144.7 41.2 %copy-start.1 = (bf16[3072,256]{1,0:T(8,128)(2,1)S(1)}, bf16[3072,256]{1,0:T(8,128)(2,1)}, u32[]{:S(2)}) copy-start(bf16[3072,256]{1,0:T(8,128)(2,1)} %param.23) | copy-start | bytes 4718596
  145.1 39.2 %copy-start.4 = (bf16[8,6144]{1,0:T(8,128)(2,1)S(1)}, bf16[8,6144]{1,0:T(8,128)(2,1)}, u32[]{:S(2)}) copy-start(bf16[8,6144]{1,0:T(8,128)(2,1)} %param.15) | copy-start | bytes 294916
Sparse Core Ops, SparseCore 0:
  63.1 16.0 all-reduce.1
